TPU v7x, 128 devices: a whole 4x4x4 slice. The times are simulated.
128 devices in a mesh: seq: 16 (over x_lo, z, core), tensor: 8 (over y, x_hi).
Axes of the slice: x: 4 (x_hi: 2, x_lo: 2; x = x_hi * 2 + x_lo), y: 4, z: 4, core: 2. Of those that a mesh axis runs over, the one named last changes fastest.
Arguments:
- tokens: bfloat16 [2048, 8192], P('seq', 'tensor'), may hold values from -2000 to 2000
- cotangent: bfloat16 [2048, 8192], P('seq', 'tensor'), may hold values from -6 to 6
- gain: float32 [8192], P('tensor'), may hold values from 0.25 to 1.75
- w_gate: bfloat16 [8192, 14336], P('tensor', 'seq'), may hold values from -0.0625 to 0.0625
- w_up: bfloat16 [8192, 14336], P('tensor', 'seq'), may hold values from -0.0625 to 0.0625
- w_down: bfloat16 [14336, 8192], P('seq', 'tensor'), may hold values from -0.046875 to 0.046875
- probe: bfloat16 [8192, 14336], P('tensor', 'seq'), may hold values from -1 to 1, as said below
Outputs:
- hessian_probe: float32 [8192, 14336], P('tensor', 'seq')
Inputs may be any that keep to these rules, and one draw needn't show every extreme that they name: `probe`: every entry is +1 or -1.
All inputs are finite; a program needn't handle non-finite values.
Results may differ from a plain program's by a relative error of at most 0.024.
Values may be sent and summed in bfloat16 or wider, within the bound.
No kernel may reach another device: no remote copies, remote signals or barrier semaphores. Data moves between devices by JAX's collectives and lax.ppermute only.
A program may use at most 128 MiB of HBM per device.

v0:
```python
import jax
import jax.numpy as jnp
from jax import lax
from jax.sharding import PartitionSpec as P

D = 8192
epsilon = 1e-05


def second_factor(pre_gate, pre_up, tangent, upstream):
    sigmoid_gate = jax.nn.sigmoid(pre_gate)
    curvature = sigmoid_gate * (1.0 - sigmoid_gate) * (2.0 + pre_gate * (1.0 - 2.0 * sigmoid_gate))
    return (upstream * pre_up * curvature * tangent).astype(jnp.bfloat16)


def body(tokens, cotangent, gain, w_gate, w_up, w_down, probe):
    gathered, upstream_rows = (
        lax.all_gather(tokens, "seq", axis=0, tiled=True),
        lax.all_gather(cotangent, "seq", axis=0, tiled=True),
    )
    values = gathered.astype(jnp.float32)
    squares = lax.psum(jnp.sum(values * values, axis=1), "tensor")
    inverse = lax.rsqrt(squares / D + epsilon)
    normed = (values * inverse[:, None] * gain[None, :]).astype(jnp.bfloat16)
    total_tokens = normed.shape[0]
    unit_count = w_gate.shape[1]
    norm_block = normed
    outputs = [
        jnp.dot(norm_block, weight, preferred_element_type=jnp.float32)
        for weight in (w_gate, w_up, probe)
    ]
    outputs.append(
        lax.dot_general(
            upstream_rows, w_down, (((1,), (1,)), ((), ())), preferred_element_type=jnp.float32
        )
    )
    summed = lax.psum_scatter(
        jnp.concatenate(outputs, axis=1).astype(jnp.bfloat16),
        "tensor",
        scatter_dimension=0,
        tiled=True,
    ).astype(jnp.float32)
    second = second_factor(
        summed[:, :unit_count],
        summed[:, unit_count : 2 * unit_count],
        summed[:, 2 * unit_count : 3 * unit_count],
        summed[:, 3 * unit_count :],
    )
    norm_block = normed
    product = lax.dot_general(
        norm_block,
        lax.all_gather(second, "tensor", axis=0, tiled=True),
        (((0,), (0,)), ((), ())),
        preferred_element_type=jnp.float32,
    )
    return product / total_tokens


def solution(mesh):
    return jax.shard_map(
        body,
        mesh=mesh,
        in_specs=(
            P("seq", "tensor"),
            P("seq", "tensor"),
            P("tensor"),
            P("tensor", "seq"),
            P("tensor", "seq"),
            P("seq", "tensor"),
            P("tensor", "seq"),
        ),
        out_specs=P("tensor", "seq"),
        check_vma=False,
    )
```

profile of v0, /device:TPU:0, one launch (start us, length us, event | category | flops | bytes accessed | tf_op | source)
XLA Modules:
  0.0 385.9 jit_solution(4910168652188962719)
XLA Ops:
  6.5 0.0 copy-start
  6.5 0.0 all-gather.4.cloned.1.call-start
  6.5 0.7 all-gather.4.cloned.1.call-update
  7.3 0.0 all-gather.6.cloned.1.call-start
  7.3 0.7 all-gather.6.cloned.1.call-update
  8.0 0.0 reduce-scatter.2.cloned.1.call-start
  8.1 40.8 %all-gather.4.cloned.1.call-done = bf16[2048,1024]{1,0:T(8,128)(2,1)} async-done(((bf16[128,1024]{1,0:T(8,128)(2,1)}), bf16[2048,1024]{1,0:T(8,128)(2,1)}) %all-gather.4.cloned.1.call-update) | async-done | bytes 4194320 | tf_op jit(solution)/shard_map/all_gather | solution.py:18
  48.9 3.1 fusion
  52.0 24.9 %psum.7 = f32[2048]{0:T(1024)S(1)} all-reduce(f32[2048]{0:T(1024)S(1)} %fusion), channel_id=1, replica_groups=mesh['seq'=16,'tensor'=8] {'tensor'}, use_global_device_ids=true, to_apply=%region_1.0 | all-reduce | flops 2048 | bytes 16384 | tf_op jit(solution)/shard_map/psum | solution.py:22
  76.9 0.0 copy-done
  76.9 0.0 copy-done.7
  76.9 0.0 copy-start.1
  77.0 0.0 copy-start.5
  77.0 8.5 %convolution_convert_fusion.2 = bf16[2048,896]{0,1:T(8,128)(2,1)} fusion(bf16[1024,896]{1,0:T(8,128)(2,1)S(1)} %copy-done, bf16[2048,1024]{1,0:T(8,128)(2,1)} %all-gather.4.cloned.1.call-done, f32[1024]{0:T(1024)S(1)} %copy-done.7, f32[2048]{0:T(1024)S(1)} %add_rsqrt_fusion), kind=kOutput, calls=%fused_computation.8 | convolution fusion | flops 3768320000 | bytes 9711616 | tf_op jit(solution)/shard_map/dot_general | solution.py:29
  85.4 0.0 copy-done.1
  85.4 0.0 copy-done.5
  85.4 6.0 %convolution_convert_fusion.1 = bf16[2048,896]{0,1:T(8,128)(2,1)} fusion(bf16[1024,896]{1,0:T(8,128)(2,1)S(1)} %copy-done.5, bf16[2048,1024]{1,0:T(8,128)(2,1)S(1)} %copy-done.1, f32[1024]{0:T(1024)S(1)} %copy-done.7, f32[2048]{0:T(1024)S(1)} %add_rsqrt_fusion), kind=kOutput, calls=%fused_computation.7 | convolution fusion | flops 3768320000 | bytes 9711616 | tf_op jit(solution)/shard_map/dot_general | solution.py:29
  91.5 0.0 copy-done.6
  91.5 5.9 %convolution_convert_fusion.3 = bf16[2048,896]{0,1:T(8,128)(2,1)} fusion(bf16[1024,896]{1,0:T(8,128)(2,1)S(1)} %copy-done.6, bf16[2048,1024]{1,0:T(8,128)(2,1)S(1)} %copy-done.1, f32[1024]{0:T(1024)S(1)} %copy-done.7, f32[2048]{0:T(1024)S(1)} %add_rsqrt_fusion), kind=kOutput, calls=%fused_computation.9 | convolution fusion | flops 3768320000 | bytes 9711616 | tf_op jit(solution)/shard_map/dot_general | solution.py:29
  97.4 6.9 %convolution_convert_fusion = bf16[2048,896]{0,1:T(8,128)(2,1)S(1)} fusion(bf16[2048,1024]{1,0:T(8,128)(2,1)} %all-gather.6.cloned.1.call-done, bf16[896,1024]{1,0:T(8,128)(2,1)} %param.12), kind=kOutput, calls=%fused_computation.6 | convolution fusion | flops 3759931392 | bytes 9699328 | tf_op jit(solution)/shard_map/dot_general | solution.py:33
  104.3 0.0 copy-done.2
  104.3 0.0 copy-done.3
  104.3 0.0 copy-done.4
  104.3 31.3 %pad_maximum_fusion = bf16[2048,3584]{0,1:T(8,128)(2,1)} fusion(bf16[2048,896]{0,1:T(8,128)(2,1)S(1)} %convolution_convert_fusion, bf16[2048,896]{0,1:T(8,128)(2,1)S(1)} %copy-done.3, bf16[2048,896]{0,1:T(8,128)(2,1)S(1)} %copy-done.2, bf16[2048,896]{0,1:T(8,128)(2,1)S(1)} %copy-done.4), kind=kLoop, calls=%fused_computation | loop fusion | flops 58720256 | bytes 29360128 | tf_op jit(solution)/shard_map/concatenate | solution.py:38
  135.6 0.0 reduce-scatter.2.cloned.1.call-update
  135.6 0.0 all-gather.8.cloned.1.call-start
  135.7 164.5 %reduce-scatter.2.cloned.1.call-done = bf16[256,3584]{0,1:T(8,128)(2,1)} async-done(((bf16[2048,3584]{0,1:T(8,128)(2,1)}), bf16[256,3584]{0,1:T(8,128)(2,1)}) %reduce-scatter.2.cloned.1.call-update) | async-done | bytes 1835024 | tf_op jit(solution)/shard_map/reduce_scatter | solution.py:37
  300.1 1.8 convert_element_type.15
  301.9 1.2 fusion.6
  303.1 0.0 all-gather.8.cloned.1.call-update
  303.2 66.1 %all-gather.8.cloned.1.call-done = bf16[2048,896]{0,1:T(8,128)(2,1)} async-done(((bf16[256,896]{0,1:T(8,128)(2,1)}), bf16[2048,896]{0,1:T(8,128)(2,1)}) %all-gather.8.cloned.1.call-update) | async-done | bytes 3670032 | tf_op jit(solution)/shard_map/all_gather | solution.py:52
  369.3 10.1 %convolution_multiply_fusion = f32[1024,896]{1,0:T(8,128)} fusion(bf16[2048,896]{0,1:T(8,128)(2,1)} %all-gather.8.cloned.1.call-done, bf16[2048,1024]{1,0:T(8,128)(2,1)} %all-gather.4.cloned.1.call-done, f32[1024]{0:T(1024)S(1)} %copy-done.7, f32[2048]{0:T(1024)S(1)} %add_rsqrt_fusion), kind=kOutput, calls=%fused_computation.10 | convolution fusion | flops 3767402496 | bytes 11546624 | tf_op jit(solution)/shard_map/dot_general | solution.py:50
  (7 shorter events, 0.0 us)
Async XLA Ops:
  6.5 70.4 %copy-start = (bf16[1024,896]{1,0:T(8,128)(2,1)S(1)}, bf16[1024,896]{1,0:T(8,128)(2,1)}, u32[]{:S(2)}) copy-start(bf16[1024,896]{1,0:T(8,128)(2,1)} %param.11) | copy-start | bytes 5505028
  6.5 70.4 %copy-start.7 = (f32[1024]{0:T(1024)S(1)}, f32[1024]{0:T(1024)}, u32[]{:S(2)}) copy-start(f32[1024]{0:T(1024)} %param.9) | copy-start | bytes 12292
  6.5 42.4 %all-gather.4.cloned.1.call-start = ((), (), s32[]{:S(2)}) async-start(), calls=%async_computation.1 | async-start | bytes 4456448 | tf_op jit(solution)/shard_map/all_gather | solution.py:18
  7.3 90.1 %all-gather.6.cloned.1.call-start = ((), (), s32[]{:S(2)}) async-start(), calls=%async_computation.2 | async-start | bytes 4456448 | tf_op jit(solution)/shard_map/all_gather | solution.py:19
  8.0 292.1 %reduce-scatter.2.cloned.1.call-start = ((), (), s32[]{:S(2)}) async-start(), calls=%async_computation.3 | async-start | bytes 16515072 | tf_op jit(solution)/shard_map/reduce_scatter | solution.py:37
  76.9 8.5 %copy-start.1 = (bf16[2048,1024]{1,0:T(8,128)(2,1)S(1)}, bf16[2048,1024]{1,0:T(8,128)(2,1)}, u32[]{:S(2)}) copy-start(bf16[2048,1024]{1,0:T(8,128)(2,1)} %all-gather.4.cloned.1.call-done) | copy-start | bytes 12582916
  77.0 8.5 %copy-start.5 = (bf16[1024,896]{1,0:T(8,128)(2,1)S(1)}, bf16[1024,896]{1,0:T(8,128)(2,1)}, u32[]{:S(2)}) copy-start(bf16[1024,896]{1,0:T(8,128)(2,1)} %param.13) | copy-start | bytes 5505028
  85.4 6.0 %copy-start.6 = (bf16[1024,896]{1,0:T(8,128)(2,1)S(1)}, bf16[1024,896]{1,0:T(8,128)(2,1)}, u32[]{:S(2)}) copy-start(bf16[1024,896]{1,0:T(8,128)(2,1)} %param.10) | copy-start | bytes 5505028
  97.4 6.9 %copy-start.2 = (bf16[2048,896]{0,1:T(8,128)(2,1)S(1)}, bf16[2048,896]{0,1:T(8,128)(2,1)}, u32[]{:S(2)}) copy-start(bf16[2048,896]{0,1:T(8,128)(2,1)} %convolution_convert_fusion.2) | copy-start | bytes 11010052
  97.4 6.9 %copy-start.3 = (bf16[2048,896]{0,1:T(8,128)(2,1)S(1)}, bf16[2048,896]{0,1:T(8,128)(2,1)}, u32[]{:S(2)}) copy-start(bf16[2048,896]{0,1:T(8,128)(2,1)} %convolution_convert_fusion.1) | copy-start | bytes 11010052
  97.4 6.9 %copy-start.4 = (bf16[2048,896]{0,1:T(8,128)(2,1)S(1)}, bf16[2048,896]{0,1:T(8,128)(2,1)}, u32[]{:S(2)}) copy-start(bf16[2048,896]{0,1:T(8,128)(2,1)} %convolution_convert_fusion.3) | copy-start | bytes 11010052
  135.6 233.7 %all-gather.8.cloned.1.call-start = ((), (), s32[]{:S(2)}) async-start(), calls=%async_computation.4 | async-start | bytes 4128768 | tf_op jit(solution)/shard_map/all_gather | solution.py:52
Sparse Core Ops, SparseCore 0:
  9.0 39.8 all-gather.3
  50.6 37.3 all-gather.5
  135.7 164.3 reduce-scatter.1
  303.3 65.9 all-gather.7
where the time goes:
time: 386 us
  waiting for transfers between devices  273 us (71%)
  other arithmetic  37.4 us (10%)
  matrix products  37.4 us (10%)
  blocking collectives  24.9 us (6%)
  between operations  13.2 us (3%)
    reduce_scatter x1, waiting for transfers between devices, body(): lax.psum_scatter(jnp.concatenate(outputs, axis=1).astype(jnp.bfloat16), '...  164 us
    all_gather x1, waiting for transfers between devices, body(): lax.all_gather(second, 'tensor', axis=0, tiled=True)  66.1 us
    all_gather x1, waiting for transfers between devices, body(): lax.all_gather(tokens, 'seq', axis=0, tiled=True)  40.8 us
    concatenate x1, other arithmetic, body(): jnp.concatenate(outputs, axis=1).astype(jnp.bfloat16)  31.3 us
    psum x1, blocking collectives, body(): squares = lax.psum(jnp.sum(values * values, axis=1), 'tensor')  24.9 us
    dot_general x3, matrix products, body(): jnp.dot(norm_block, weight, preferred_element_type=jnp.float32)  20.4 us
    dot_general x1, matrix products, body(): lax.dot_general(norm_block, lax.all_gather(second, 'tensor', axis=0, tile...  10.1 us
  transfers between devices with their start and end apart: 4, of which 3 were waited for; matrix products, arithmetic and copies ran while one was open for 6% of the time, Pallas kernels for 0%

commit v1 on v0

--- a/solution.py
+++ b/solution.py
@@ -15,7 +15,9 @@
 
 def body(tokens, cotangent, gain, w_gate, w_up, w_down, probe):
     gathered, upstream_rows = (
-        lax.all_gather(tokens, "seq", axis=0, tiled=True),
+        jnp.concatenate(
+            lax.all_to_all(jnp.stack([tokens] * lax.axis_size("seq")), "seq", 0, 0), axis=0
+        ),
         lax.all_gather(cotangent, "seq", axis=0, tiled=True),
     )
     values = gathered.astype(jnp.float32)

time: 386 us -> 417 us (1.080)
  blocking collectives: 24.9 us -> 98.9 us
  waiting for transfers between devices: 273 us -> 230 us
  matrix products: 37.4 us -> 33.2 us
    all_to_all x0 -> x1, blocking collectives: none -> 74.3 us  [body(): lax.all_to_all(jnp.stack([tokens] * lax.axis_size('seq')), 'seq', 0, 0)]
    all_gather x1 -> x0, waiting for transfers between devices: 40.8 us -> none  [body(): lax.all_gather(tokens, 'seq', axis=0, tiled=True)]
  transfers between devices with their start and end apart: 4 -> 3, of which waited for: 3 -> 2; matrix products, arithmetic and copies ran while one was open for 6% -> 5% of each run, Pallas kernels for 0% -> 0%
where the time goes in v1:
time: 417 us
  waiting for transfers between devices  230 us (55%)
  blocking collectives  98.9 us (24%)
  other arithmetic  37.9 us (9%)
  matrix products  33.2 us (8%)
  between operations  13.2 us (3%)
    reduce_scatter x1, waiting for transfers between devices, body(): lax.psum_scatter(jnp.concatenate(outputs, axis=1).astype(jnp.bfloat16), '...  163 us
    all_to_all x1, blocking collectives, body(): lax.all_to_all(jnp.stack([tokens] * lax.axis_size('seq')), 'seq', 0, 0)  74.3 us
    all_gather x1, waiting for transfers between devices, body(): lax.all_gather(second, 'tensor', axis=0, tiled=True)  66.2 us
    concatenate x1, other arithmetic, body(): jnp.concatenate(outputs, axis=1).astype(jnp.bfloat16)  31.2 us
    psum x1, blocking collectives, body(): squares = lax.psum(jnp.sum(values * values, axis=1), 'tensor')  24.6 us
    dot_general x3, matrix products, body(): jnp.dot(norm_block, weight, preferred_element_type=jnp.float32)  16.4 us
    dot_general x1, matrix products, body(): lax.dot_general(norm_block, lax.all_gather(second, 'tensor', axis=0, tile...  9.81 us
  transfers between devices with their start and end apart: 3, of which 2 were waited for; matrix products, arithmetic and copies ran while one was open for 5% of the time, Pallas kernels for 0%

profile of v1, /device:TPU:0, one launch (start us, length us, event | category | flops | bytes accessed | tf_op | source)
XLA Modules:
  0.0 416.7 jit_solution(6610163469404868983)
XLA Ops:
  6.5 0.0 copy-start
  6.5 0.0 all-gather.3.cloned.1.call-start
  6.5 0.7 all-gather.3.cloned.1.call-update
  7.3 0.0 reduce-scatter.2.cloned.1.call-start
  7.3 1.5 stack.2
  8.8 74.3 %all_to_all.5 = bf16[16,128,1024]{2,1,0:T(8,128)(2,1)S(1)} all-to-all(bf16[16,128,1024]{2,1,0:T(8,128)(2,1)S(1)} %stack.2), channel_id=1, replica_groups=mesh['seq'=16,'tensor'=8] {'seq'}, dimensions={0} | all-to-all | bytes 8388608 | tf_op jit(solution)/shard_map/all_to_all | solution.py:19
  83.1 2.0 copy-done.2
  85.1 0.9 multiply_reduce_fusion
  86.0 24.6 %psum.7 = f32[2048]{0:T(1024)S(1)} all-reduce(f32[2048]{0:T(1024)S(1)} %bitcast.17), channel_id=1, replica_groups=mesh['seq'=16,'tensor'=8] {'tensor'}, use_global_device_ids=true, to_apply=%region_1.0 | all-reduce | flops 2048 | bytes 16384 | tf_op jit(solution)/shard_map/psum | solution.py:24
  110.5 0.0 copy-done.7
  110.6 2.8 fusion.1
  113.4 0.0 copy-done
  113.4 0.0 copy-start.3
  113.4 0.0 copy-start.8
  113.4 5.5 %convolution_convert_fusion.1 = bf16[2048,896]{0,1:T(8,128)(2,1)} fusion(bf16[2048,1024]{1,0:T(8,128)(2,1)S(1)} %fusion.1, bf16[1024,896]{1,0:T(8,128)(2,1)S(1)} %copy-done), kind=kOutput, calls=%fused_computation.6 | convolution fusion | flops 3759931392 | bytes 9699328 | tf_op jit(solution)/shard_map/dot_general | solution.py:31
  118.9 0.0 copy-done.8
  118.9 5.5 %convolution_convert_fusion.2 = bf16[2048,896]{0,1:T(8,128)(2,1)} fusion(bf16[2048,1024]{1,0:T(8,128)(2,1)S(1)} %fusion.1, bf16[1024,896]{1,0:T(8,128)(2,1)S(1)} %copy-done.8), kind=kOutput, calls=%fused_computation.7 | convolution fusion | flops 3759931392 | bytes 9699328 | tf_op jit(solution)/shard_map/dot_general | solution.py:31
  124.4 0.0 copy-done.3
  124.4 0.0 copy-done.9
  124.4 5.5 %convolution_convert_fusion.3 = bf16[2048,896]{0,1:T(8,128)(2,1)} fusion(bf16[2048,1024]{1,0:T(8,128)(2,1)S(1)} %fusion.1, bf16[1024,896]{1,0:T(8,128)(2,1)S(1)} %copy-done.9), kind=kOutput, calls=%fused_computation.8 | convolution fusion | flops 3759931392 | bytes 9699328 | tf_op jit(solution)/shard_map/dot_general | solution.py:31
  129.9 6.9 %convolution_convert_fusion = bf16[2048,896]{0,1:T(8,128)(2,1)S(1)} fusion(bf16[2048,1024]{1,0:T(8,128)(2,1)} %all-gather.3.cloned.1.call-done, bf16[896,1024]{1,0:T(8,128)(2,1)} %param.12), kind=kOutput, calls=%fused_computation.5 | convolution fusion | flops 3759931392 | bytes 9699328 | tf_op jit(solution)/shard_map/dot_general | solution.py:35
  136.8 0.0 copy-done.4
  136.8 0.0 copy-done.5
  136.8 31.2 %pad_maximum_fusion = bf16[2048,3584]{0,1:T(8,128)(2,1)} fusion(bf16[2048,896]{0,1:T(8,128)(2,1)S(1)} %convolution_convert_fusion, bf16[2048,896]{0,1:T(8,128)(2,1)S(1)} %copy-done.4, bf16[2048,896]{0,1:T(8,128)(2,1)S(1)} %copy-done.5, bf16[2048,896]{0,1:T(8,128)(2,1)S(1)} %copy-done.6), kind=kLoop, calls=%fused_computation | loop fusion | flops 58720256 | bytes 29360128 | tf_op jit(solution)/shard_map/concatenate | solution.py:40
  168.0 0.0 reduce-scatter.2.cloned.1.call-update
  168.1 0.0 all-gather.5.cloned.1.call-start
  168.1 163.0 %reduce-scatter.2.cloned.1.call-done = bf16[256,3584]{0,1:T(8,128)(2,1)} async-done(((bf16[2048,3584]{0,1:T(8,128)(2,1)}), bf16[256,3584]{0,1:T(8,128)(2,1)}) %reduce-scatter.2.cloned.1.call-update) | async-done | bytes 1835024 | tf_op jit(solution)/shard_map/reduce_scatter | solution.py:39
  331.1 1.8 convert_element_type.23
  332.9 1.2 fusion.5
  334.2 0.0 all-gather.5.cloned.1.call-update
  334.2 66.2 %all-gather.5.cloned.1.call-done = bf16[2048,896]{0,1:T(8,128)(2,1)} async-done(((bf16[256,896]{0,1:T(8,128)(2,1)}), bf16[2048,896]{0,1:T(8,128)(2,1)}) %all-gather.5.cloned.1.call-update) | async-done | bytes 3670032 | tf_op jit(solution)/shard_map/all_gather | solution.py:54
  400.3 9.8 %convolution_multiply_fusion = f32[1024,896]{1,0:T(8,128)} fusion(bf16[2048,1024]{1,0:T(8,128)(2,1)} %copy-done.3, bf16[2048,896]{0,1:T(8,128)(2,1)} %all-gather.5.cloned.1.call-done), kind=kOutput, calls=%fused_computation.9 | convolution fusion | flops 3759013888 | bytes 11534336 | tf_op jit(solution)/shard_map/dot_general | solution.py:52
  (11 shorter events, 0.0 us)
Async XLA Ops:
  6.5 106.8 %copy-start = (bf16[1024,896]{1,0:T(8,128)(2,1)S(1)}, bf16[1024,896]{1,0:T(8,128)(2,1)}, u32[]{:S(2)}) copy-start(bf16[1024,896]{1,0:T(8,128)(2,1)} %param.13) | copy-start | bytes 5505028
  6.5 123.3 %all-gather.3.cloned.1.call-start = ((), (), s32[]{:S(2)}) async-start(), calls=%async_computation.2 | async-start | bytes 4456448 | tf_op jit(solution)/shard_map/all_gather | solution.py:21
  7.3 323.9 %reduce-scatter.2.cloned.1.call-start = ((), (), s32[]{:S(2)}) async-start(), calls=%async_computation.3 | async-start | bytes 16515072 | tf_op jit(solution)/shard_map/reduce_scatter | solution.py:39
  83.1 2.0 copy-start.2
  85.1 25.5 %copy-start.7 = (f32[1024]{0:T(1024)S(1)}, f32[1024]{0:T(1024)}, u32[]{:S(2)}) copy-start(f32[1024]{0:T(1024)} %param.9) | copy-start | bytes 12292
  113.4 11.0 %copy-start.3 = (bf16[2048,1024]{1,0:T(8,128)(2,1)}, bf16[2048,1024]{1,0:T(8,128)(2,1)S(1)}, u32[]{:S(2)}) copy-start(bf16[2048,1024]{1,0:T(8,128)(2,1)S(1)} %fusion.1) | copy-start | bytes 12582916
  113.4 5.5 %copy-start.8 = (bf16[1024,896]{1,0:T(8,128)(2,1)S(1)}, bf16[1024,896]{1,0:T(8,128)(2,1)}, u32[]{:S(2)}) copy-start(bf16[1024,896]{1,0:T(8,128)(2,1)} %param.11) | copy-start | bytes 5505028
  118.9 5.5 %copy-start.9 = (bf16[1024,896]{1,0:T(8,128)(2,1)S(1)}, bf16[1024,896]{1,0:T(8,128)(2,1)}, u32[]{:S(2)}) copy-start(bf16[1024,896]{1,0:T(8,128)(2,1)} %param.10) | copy-start | bytes 5505028
  129.8 6.9 %copy-start.4 = (bf16[2048,896]{0,1:T(8,128)(2,1)S(1)}, bf16[2048,896]{0,1:T(8,128)(2,1)}, u32[]{:S(2)}) copy-start(bf16[2048,896]{0,1:T(8,128)(2,1)} %convolution_convert_fusion.1) | copy-start | bytes 11010052
  129.8 6.9 %copy-start.5 = (bf16[2048,896]{0,1:T(8,128)(2,1)S(1)}, bf16[2048,896]{0,1:T(8,128)(2,1)}, u32[]{:S(2)}) copy-start(bf16[2048,896]{0,1:T(8,128)(2,1)} %convolution_convert_fusion.2) | copy-start | bytes 11010052
  129.9 6.9 %copy-start.6 = (bf16[2048,896]{0,1:T(8,128)(2,1)S(1)}, bf16[2048,896]{0,1:T(8,128)(2,1)}, u32[]{:S(2)}) copy-start(bf16[2048,896]{0,1:T(8,128)(2,1)} %convolution_convert_fusion.3) | copy-start | bytes 11010052
  168.1 232.3 %all-gather.5.cloned.1.call-start = ((), (), s32[]{:S(2)}) async-start(), calls=%async_computation.4 | async-start | bytes 4128768 | tf_op jit(solution)/shard_map/all_gather | solution.py:54
  400.3 9.8 %copy-start.1 = (bf16[1024,896]{1,0:T(8,128)(2,1)S(1)}, bf16[1024,896]{1,0:T(8,128)(2,1)}, u32[]{:S(2)}) copy-start(bf16[1024,896]{1,0:T(8,128)(2,1)} %param.13) | copy-start | bytes 5505028
Sparse Core Ops, SparseCore 0:
  9.0 76.2 all-gather.2
  168.2 162.9 reduce-scatter.1
  334.3 65.9 all-gather.4
